TPU v7x, 256 devices: a whole 4x4x8 slice. The times are simulated.
256 devices in a mesh: rows: 256 (over x, y, z, core).
Axes of the slice: x: 4, y: 4, z: 8, core: 2. Of those that a mesh axis runs over, the one named last changes fastest.
Arguments:
- hamiltonian: float32 [393216, 1728], P('rows'), may hold values from -0.15625 to 0.15625
- subspace: float32 [393216, 128], P('rows'), may hold values from -6 to 6
- block_cols: int32 [6144, 27], P('rows'), may hold values from 0 to 6151, as said below
- far_list: int32 [256, 8], P('rows'), may hold values from -1 to 6143, as said below
Outputs:
- filtered: float32 [393216, 128], P('rows')
Inputs may be any that keep to these rules, and one draw needn't show every extreme that they name: `far_list`: row d holds in slots 0 to c_d - 1 distinct block indices owned by device d xor (32) (that device owns blocks k * 24 to k * 24 + 23 for its index k), and -1 in its other slots; c_d is 2 or more, and device 0 fills all 8 slots. `block_cols`: entry 0 of row i is i; the next 24 entries are distinct blocks (i + o) mod 6144 with 0 < |o| <= 13; the last two are 6144 + s for two distinct filled slots s of far_list's row of the device that owns row i.
All inputs are finite; a program needn't handle non-finite values.
Results may differ from a plain program's by a relative error of at most 0.000058.
Values sent between devices are 32-bit elements; how exact they have to be, the bound alone decides.
A program may use at most 128 MiB of HBM per device.

v0:
```python
import jax
import jax.numpy as jnp
from jax import lax
from jax.sharding import PartitionSpec as P

CENTER = 0.25
HALF_WIDTH = 1.5


def partner(value, axis, bit):
    mask = 2**bit
    pairs = [(source, source ^ mask) for source in range(lax.axis_size(axis))]
    return lax.ppermute(value, axis, pairs)


def extended_2(value, sides, width):
    for axis, dim in sides:
        devices, length = (lax.axis_size(axis), value.shape[dim])
        up = [(i, (i + 1) % devices) for i in range(devices)]
        down = [(j, i) for i, j in up]
        last = lax.slice_in_dim(value, length - width, length, axis=dim)
        leading = lax.slice_in_dim(value, 0, width, axis=dim)
        before = lax.ppermute(last, axis, up)
        after = lax.ppermute(leading, axis, down)
        value = jnp.concatenate([before, value, after], axis=dim)
    return value


def gather_blocks(extended, positions, block_size):
    sub_width = extended.shape[1]
    blocks = extended.reshape(-1, block_size, sub_width)
    picked = blocks[positions]
    return picked.reshape(positions.shape[0], positions.shape[1] * block_size, sub_width)


def per_device(hamiltonian, subspace, block_cols, far_list):
    block_rows, entries = block_cols.shape
    block_size = hamiltonian.shape[1] // entries
    sub_width = subspace.shape[1]
    slot_total = far_list.shape[1]
    device_count = lax.axis_size("rows")
    my_index = lax.axis_index("rows")
    block_total = block_rows * device_count
    swap_level = (device_count // 8).bit_length() - 1
    first_row = my_index * block_rows
    inband = block_cols < block_total
    slot_index = jnp.clip(block_cols - block_total, 0, slot_total - 1)
    asked_list = partner(far_list, "rows", swap_level)
    valid_mask = (asked_list[0] >= 0).astype(jnp.float32)
    local_index = jnp.clip(asked_list[0] - first_row, 0, block_rows - 1)
    band_count = block_rows + 2 * block_rows
    positions = jnp.where(
        inband, (block_cols - first_row + block_rows) % block_total, band_count + slot_index
    )
    ham_slab = hamiltonian.reshape(block_rows, block_size, entries * block_size)

    def apply_operator(vectors):
        band_panel = extended_2(vectors, (("rows", 0),), block_rows * block_size)
        outgoing = (
            vectors.reshape(block_rows, block_size, sub_width)[local_index]
            * valid_mask[:, None, None]
        )
        remote = partner(outgoing.reshape(slot_total * block_size, sub_width), "rows", swap_level)
        extended = jnp.concatenate([band_panel, remote], axis=0)
        picked = gather_blocks(extended, positions, block_size)
        result = jnp.einsum("irm,imk->irk", ham_slab, picked, precision=lax.Precision.HIGHEST)
        return result.reshape(block_rows * block_size, sub_width)

    first_term = (apply_operator(subspace) - CENTER * subspace) / HALF_WIDTH
    second = apply_operator(first_term)
    return 2.0 / HALF_WIDTH * (second - CENTER * first_term) - subspace


def solution(mesh):
    placed = (P("rows", None), P("rows", None), P("rows", None), P("rows", None))
    return jax.shard_map(
        per_device, mesh=mesh, in_specs=placed, out_specs=P("rows", None), check_vma=False
    )
```

profile of v0, /device:TPU:1, one launch (start us, length us, event | category | flops | bytes accessed | tf_op | source)
XLA Modules:
  0.0 118.4 jit_solution(9992738143636502731)
XLA Ops:
  0.0 3.2 %collective-permute-start.1 = (f32[1536,128]{1,0:T(8,128)}, f32[1536,128]{1,0:T(8,128)S(1)}, u32[]{:S(2)}, u32[]{:S(2)}) collective-permute-start(f32[1536,128]{1,0:T(8,128)} %param.5), channel_id=1, source_target_pairs={{1,0},{2,1},{3,2},{4,3},{5,4},{6,5},{7,6},{8,7},{9,8},{10,9},{11,1... | collective-permute-start | bytes 2359304 | tf_op jit(solution)/shard_map/ppermute | solution.py:24
  3.2 2.7 %collective-permute-start.2 = (s32[1,8]{1,0:T(1,128)}, s32[1,8]{1,0:T(1,128)S(1)}, u32[]{:S(2)}, u32[]{:S(2)}) collective-permute-start(s32[1,8]{1,0:T(1,128)} %param.7), channel_id=1, source_target_pairs={{0,32},{1,33},{2,34},{3,35},{4,36},{5,37},{6,38},{7,39},{8,40},{9,... | collective-permute-start | bytes 104 | tf_op jit(solution)/shard_map/ppermute | solution.py:13
  5.9 1.3 %collective-permute-done.2 = s32[1,8]{1,0:T(1,128)S(1)} collective-permute-done((s32[1,8]{1,0:T(1,128)}, s32[1,8]{1,0:T(1,128)S(1)}, u32[]{:S(2)}, u32[]{:S(2)}) %collective-permute-start.2) | collective-permute-done | bytes 64 | tf_op jit(solution)/shard_map/ppermute | solution.py:13
  7.4 1.7 %gather_fusion = f32[8,64,128]{2,1,0:T(8,128)S(1)} fusion(f32[24,64,128]{2,1,0:T(8,128)} %bitcast.43, s32[1024]{0:T(1024)S(1)} %pad_clamp_fusion.1), kind=kCustom, calls=%fused_computation | custom fusion | bytes 524320 | tf_op jit(solution)/shard_map/gather | solution.py:60
  9.2 0.1 bitcast_multiply_fusion.1
  9.3 2.8 %collective-permute-start.3 = (f32[512,128]{1,0:T(8,128)S(1)}, f32[512,128]{1,0:T(8,128)S(1)}, u32[]{:S(2)}, u32[]{:S(2)}) collective-permute-start(f32[512,128]{1,0:T(8,128)S(1)} %bitcast_multiply_fusion.1), channel_id=1, source_target_pairs={{0,32},{1,33},{2,34},{3,35},{4,36},{5,37},{6,38},{7,39},{8,40},{9,... | collective-permute-start | bytes 786440 | tf_op jit(solution)/shard_map/ppermute | solution.py:13
  12.1 0.7 compare_select_fusion
  12.9 11.8 %copy.7 = f32[1536,1728]{1,0:T(8,128)} copy(f32[1536,1728]{0,1:T(8,128)} %param.4) | data formatting | bytes 21233664 | tf_op args[0]
  24.7 2.6 %collective-permute-done.3 = f32[512,128]{1,0:T(8,128)S(1)} collective-permute-done((f32[512,128]{1,0:T(8,128)S(1)}, f32[512,128]{1,0:T(8,128)S(1)}, u32[]{:S(2)}, u32[]{:S(2)}) %collective-permute-start.3) | collective-permute-done | bytes 262176 | tf_op jit(solution)/shard_map/ppermute | solution.py:13
  27.2 0.7 copy-done.5
  27.9 0.9 copy-done.3
  28.8 1.6 %pad_maximum_fusion = f32[5120,128]{1,0:T(8,128)S(1)} fusion(f32[512,128]{1,0:T(8,128)} %copy-done.5, f32[1536,128]{1,0:T(8,128)} %copy-done.3, f32[1536,128]{1,0:T(8,128)S(1)} %copy-done, f32[1536,128]{1,0:T(8,128)} %collective-permute-done), kind=kLoop, calls=%fused_computation.4 | loop fusion | flops 1966080 | bytes 5242880 | tf_op jit(solution)/shard_map/concatenate | solution.py:64
  30.5 8.3 %gather_fusion.1 = f32[648,64,128]{2,1,0:T(8,128)} fusion(f32[80,64,128]{2,1,0:T(8,128)S(1)} %bitcast.40, s32[1024]{0:T(1024)S(1)} %pad_clamp_fusion), kind=kCustom, calls=%fused_computation.1 | custom fusion | bytes 42469920 | tf_op jit(solution)/shard_map/gather | solution.py:32
  38.8 18.1 %fusion.9 = f32[24,128,64]{1,2,0:T(8,128)S(1)} fusion(f32[24,1728,128]{2,1,0:T(8,128)} %bitcast.42, f32[24,64,1728]{2,1,0:T(8,128)} %bitcast.37), kind=kOutput, calls=%fused_computation.26 | convolution fusion | flops 4076863488 | bytes 32636928 | tf_op jit(solution)/shard_map/irm,imk->irk/dot_general | solution.py:66
  57.0 11.0 %collective-permute-start.5 = (f32[1536,128]{1,0:T(8,128)S(1)}, f32[1536,128]{1,0:T(8,128)S(1)}, u32[]{:S(2)}, u32[]{:S(2)}) collective-permute-start(f32[1536,128]{1,0:T(8,128)S(1)} %fusion.2), channel_id=1, source_target_pairs={{1,0},{2,1},{3,2},{4,3},{5,4},{6,5},{7,6},{8,7},{9,8},{10,9},{11,1... | collective-permute-start | bytes 2359304 | tf_op jit(solution)/shard_map/ppermute | solution.py:24
  68.0 0.6 gather_fusion.2
  68.5 0.1 bitcast_multiply_fusion
  68.7 3.5 %collective-permute-start.6 = (f32[512,128]{1,0:T(8,128)S(1)}, f32[512,128]{1,0:T(8,128)S(1)}, u32[]{:S(2)}, u32[]{:S(2)}) collective-permute-start(f32[512,128]{1,0:T(8,128)S(1)} %bitcast_multiply_fusion), channel_id=1, source_target_pairs={{0,32},{1,33},{2,34},{3,35},{4,36},{5,37},{6,38},{7,39},{8,40},{9,... | collective-permute-start | bytes 786440 | tf_op jit(solution)/shard_map/ppermute | solution.py:13
  72.2 15.8 %collective-permute-done.6 = f32[512,128]{1,0:T(8,128)S(1)} collective-permute-done((f32[512,128]{1,0:T(8,128)S(1)}, f32[512,128]{1,0:T(8,128)S(1)}, u32[]{:S(2)}, u32[]{:S(2)}) %collective-permute-start.6) | collective-permute-done | bytes 262176 | tf_op jit(solution)/shard_map/ppermute | solution.py:13
  88.0 0.9 copy-done.4
  88.9 1.8 %pad_maximum_fusion.1 = f32[5120,128]{1,0:T(8,128)S(1)} fusion(f32[512,128]{1,0:T(8,128)S(1)} %collective-permute-done.6, f32[1536,128]{1,0:T(8,128)} %copy-done.4, f32[1536,128]{1,0:T(8,128)} %copy-done.2, f32[1536,128]{1,0:T(8,128)} %collective-permute-done.4), kind=kLoop, calls=%fused_computation.5 | loop fusion | flops 1966080 | bytes 5242880 | tf_op jit(solution)/shard_map/concatenate | solution.py:64
  90.7 8.3 %gather_fusion.3 = f32[648,64,128]{2,1,0:T(8,128)} fusion(f32[80,64,128]{2,1,0:T(8,128)S(1)} %bitcast.39, s32[1024]{0:T(1024)S(1)} %pad_clamp_fusion), kind=kCustom, calls=%fused_computation.3 | custom fusion | bytes 42469920 | tf_op jit(solution)/shard_map/gather | solution.py:32
  99.0 18.4 %fusion.10 = f32[24,128,64]{1,2,0:T(8,128)S(1)} fusion(f32[24,1728,128]{2,1,0:T(8,128)} %bitcast.41, f32[24,64,1728]{2,1,0:T(8,128)} %bitcast.38), kind=kOutput, calls=%fused_computation.27 | convolution fusion | flops 4076863488 | bytes 32636928 | tf_op jit(solution)/shard_map/irm,imk->irk/dot_general | solution.py:66
  117.4 1.1 fusion.1
  (23 shorter events, 0.4 us)
Async XLA Ops:
  0.0 27.2 %collective-permute-start.1 = (f32[1536,128]{1,0:T(8,128)}, f32[1536,128]{1,0:T(8,128)S(1)}, u32[]{:S(2)}, u32[]{:S(2)}) collective-permute-start(f32[1536,128]{1,0:T(8,128)} %param.5), channel_id=1, source_target_pairs={{1,0},{2,1},{3,2},{4,3},{5,4},{6,5},{7,6},{8,7},{9,8},{10,9},{11,1... | collective-permute-start | bytes 2359304 | tf_op jit(solution)/shard_map/ppermute | solution.py:24
  3.2 25.6 %collective-permute-start = (f32[1536,128]{1,0:T(8,128)}, f32[1536,128]{1,0:T(8,128)}, u32[]{:S(2)}, u32[]{:S(2)}) collective-permute-start(f32[1536,128]{1,0:T(8,128)} %param.5), channel_id=1, source_target_pairs={{0,1},{1,2},{2,3},{3,4},{4,5},{5,6},{6,7},{7,8},{8,9},{9,10},{10,1... | collective-permute-start | bytes 2359304 | tf_op jit(solution)/shard_map/ppermute | solution.py:23
  3.2 4.0 %collective-permute-start.2 = (s32[1,8]{1,0:T(1,128)}, s32[1,8]{1,0:T(1,128)S(1)}, u32[]{:S(2)}, u32[]{:S(2)}) collective-permute-start(s32[1,8]{1,0:T(1,128)} %param.7), channel_id=1, source_target_pairs={{0,32},{1,33},{2,34},{3,35},{4,36},{5,37},{6,38},{7,39},{8,40},{9,... | collective-permute-start | bytes 104 | tf_op jit(solution)/shard_map/ppermute | solution.py:13
  9.1 19.7 %copy-start = (f32[1536,128]{1,0:T(8,128)S(1)}, f32[1536,128]{1,0:T(8,128)}, u32[]{:S(2)}) copy-start(f32[1536,128]{1,0:T(8,128)} %param.5) | copy-start | bytes 2359300
  9.3 17.9 %collective-permute-start.3 = (f32[512,128]{1,0:T(8,128)S(1)}, f32[512,128]{1,0:T(8,128)S(1)}, u32[]{:S(2)}, u32[]{:S(2)}) collective-permute-start(f32[512,128]{1,0:T(8,128)S(1)} %bitcast_multiply_fusion.1), channel_id=1, source_target_pairs={{0,32},{1,33},{2,34},{3,35},{4,36},{5,37},{6,38},{7,39},{8,40},{9,... | collective-permute-start | bytes 786440 | tf_op jit(solution)/shard_map/ppermute | solution.py:13
  27.2 0.7 copy-start.5
  27.9 0.9 copy-start.3
  57.0 31.0 %copy-start.2 = (f32[1536,128]{1,0:T(8,128)}, f32[1536,128]{1,0:T(8,128)S(1)}, u32[]{:S(2)}) copy-start(f32[1536,128]{1,0:T(8,128)S(1)} %fusion.2) | copy-start | bytes 2359300
  57.0 31.0 %collective-permute-start.5 = (f32[1536,128]{1,0:T(8,128)S(1)}, f32[1536,128]{1,0:T(8,128)S(1)}, u32[]{:S(2)}, u32[]{:S(2)}) collective-permute-start(f32[1536,128]{1,0:T(8,128)S(1)} %fusion.2), channel_id=1, source_target_pairs={{1,0},{2,1},{3,2},{4,3},{5,4},{6,5},{7,6},{8,7},{9,8},{10,9},{11,1... | collective-permute-start | bytes 2359304 | tf_op jit(solution)/shard_map/ppermute | solution.py:24
  68.0 20.9 %collective-permute-start.4 = (f32[1536,128]{1,0:T(8,128)S(1)}, f32[1536,128]{1,0:T(8,128)}, u32[]{:S(2)}, u32[]{:S(2)}) collective-permute-start(f32[1536,128]{1,0:T(8,128)S(1)} %fusion.2), channel_id=1, source_target_pairs={{0,1},{1,2},{2,3},{3,4},{4,5},{5,6},{6,7},{7,8},{8,9},{9,10},{10,1... | collective-permute-start | bytes 2359304 | tf_op jit(solution)/shard_map/ppermute | solution.py:23
  68.7 19.3 %collective-permute-start.6 = (f32[512,128]{1,0:T(8,128)S(1)}, f32[512,128]{1,0:T(8,128)S(1)}, u32[]{:S(2)}, u32[]{:S(2)}) collective-permute-start(f32[512,128]{1,0:T(8,128)S(1)} %bitcast_multiply_fusion), channel_id=1, source_target_pairs={{0,32},{1,33},{2,34},{3,35},{4,36},{5,37},{6,38},{7,39},{8,40},{9,... | collective-permute-start | bytes 786440 | tf_op jit(solution)/shard_map/ppermute | solution.py:13
  88.0 0.9 copy-start.4
  99.0 18.4 %copy-start.1 = (f32[1536,128]{1,0:T(8,128)S(1)}, f32[1536,128]{1,0:T(8,128)}, u32[]{:S(2)}) copy-start(f32[1536,128]{1,0:T(8,128)} %param.5) | copy-start | bytes 2359300
where the time goes:
time: 119 us; the launch traced here: 118 us
  matrix products  36.4 us (31%)
  local copies, waits for them, and re-layouts  33.4 us (28%)
  starting transfers between devices  23.2 us (19%)
  waiting for transfers between devices  19.7 us (17%)
  other arithmetic  5.57 us (5%)
    dot_general x2, matrix products, apply_operator(): jnp.einsum('irm,imk->irk', ham_slab, picked, precision=lax.Precision.HIGH...  36.4 us
    ppermute x3, waiting for transfers between devices, partner(): return lax.ppermute(value, axis, pairs)  19.7 us
    gather x2, local copies, waits for them, and re-layouts, gather_blocks(): picked = blocks[positions]  16.7 us
    unnamed x13, local copies, waits for them, and re-layouts  14.2 us
    ppermute x2, starting transfers between devices, extended_2(): after = lax.ppermute(leading, axis, down)  14.2 us
    ppermute x3, starting transfers between devices, partner(): return lax.ppermute(value, axis, pairs)  8.99 us
    concatenate x2, other arithmetic, apply_operator(): extended = jnp.concatenate([band_panel, remote], axis=0)  3.4 us
  transfers between devices with their start and end apart: 7, of which 3 were waited for; matrix products, arithmetic and copies ran while one was open for 13% of the time, Pallas kernels for 0%

commit v1 on v0

v1 whole, which is shorter than its diff:
```python
import functools

import jax
import jax.numpy as jnp
from jax import lax
from jax.experimental import pallas as pl
from jax.experimental.pallas import tpu as pltpu
from jax.sharding import PartitionSpec as P

CENTER = 0.25
HALF_WIDTH = 1.5
REACH = 13
ROWS_PER_STEP = 4


def partner(value, axis, bit):
    mask = 2**bit
    pairs = [(source, source ^ mask) for source in range(lax.axis_size(axis))]
    return lax.ppermute(value, axis, pairs)


def halo(value, axis, width):
    devices, length = lax.axis_size(axis), value.shape[0]
    up = [(i, (i + 1) % devices) for i in range(devices)]
    down = [(j, i) for i, j in up]
    before = lax.ppermute(value[length - width:], axis, up)
    after = lax.ppermute(value[:width], axis, down)
    return before, after


def apply_kernel(mode, entries, block_size, pos_ref, ham_ref, ext_ref, own_ref, *rest):
    if mode == 0:
        (out_ref,) = rest
    else:
        base_ref, out_ref = rest
    step = pl.program_id(0)
    rows = ham_ref.shape[0] // block_size
    for r in range(rows):
        i = step * rows + r
        pieces = []
        for j in range(entries):
            start = pl.multiple_of(pos_ref[i * entries + j] * block_size, block_size)
            pieces.append(ext_ref[pl.ds(start, block_size), :])
        panel = jnp.concatenate(pieces, axis=0)
        acc = jnp.dot(
            ham_ref[r * block_size:(r + 1) * block_size, :],
            panel,
            precision=lax.Precision.HIGHEST,
            preferred_element_type=jnp.float32,
        )
        rs = slice(r * block_size, (r + 1) * block_size)
        own = own_ref[rs, :]
        if mode == 0:
            out_ref[rs, :] = (acc - CENTER * own) / HALF_WIDTH
        else:
            out_ref[rs, :] = 2.0 / HALF_WIDTH * (acc - CENTER * own) - base_ref[rs, :]


def block_apply(mode, entries, positions, hamiltonian, extended, own, base=None):
    block_size = hamiltonian.shape[1] // entries
    block_rows = own.shape[0] // block_size
    step_rows = ROWS_PER_STEP * block_size
    steps = block_rows // ROWS_PER_STEP
    width = own.shape[1]
    in_specs = [
        pl.BlockSpec((step_rows, hamiltonian.shape[1]), lambda s, pos: (s, 0)),
        pl.BlockSpec(extended.shape, lambda s, pos: (0, 0)),
        pl.BlockSpec((step_rows, width), lambda s, pos: (s, 0)),
    ]
    args = [hamiltonian, extended, own]
    if mode == 1:
        in_specs.append(pl.BlockSpec((step_rows, width), lambda s, pos: (s, 0)))
        args.append(base)
    flops = 2 * hamiltonian.shape[0] * hamiltonian.shape[1] * width
    return pl.pallas_call(
        functools.partial(apply_kernel, mode, entries, block_size),
        out_shape=jax.ShapeDtypeStruct(own.shape, jnp.float32),
        grid_spec=pltpu.PrefetchScalarGridSpec(
            num_scalar_prefetch=1,
            grid=(steps,),
            in_specs=in_specs,
            out_specs=pl.BlockSpec((step_rows, width), lambda s, pos: (s, 0)),
        ),
        compiler_params=pltpu.CompilerParams(vmem_limit_bytes=48 * 1024 * 1024),
        cost_estimate=pl.CostEstimate(
            flops=6 * flops,
            transcendentals=0,
            bytes_accessed=4 * (hamiltonian.size + extended.size + 3 * own.size),
        ),
    )(positions, *args)


def per_device(hamiltonian, subspace, block_cols, far_list):
    block_rows, entries = block_cols.shape
    block_size = hamiltonian.shape[1] // entries
    sub_width = subspace.shape[1]
    slot_total = far_list.shape[1]
    device_count = lax.axis_size("rows")
    my_index = lax.axis_index("rows")
    block_total = block_rows * device_count
    swap_level = (device_count // 8).bit_length() - 1
    first_row = my_index * block_rows
    inband = block_cols < block_total
    slot_index = jnp.clip(block_cols - block_total, 0, slot_total - 1)
    asked_list = partner(far_list, "rows", swap_level)
    valid_mask = (asked_list[0] >= 0).astype(jnp.float32)
    local_index = jnp.clip(asked_list[0] - first_row, 0, block_rows - 1)
    band_count = block_rows + 2 * REACH
    positions = jnp.where(
        inband, (block_cols - first_row + REACH) % block_total, band_count + slot_index
    )
    positions = jnp.clip(positions, 0, band_count + slot_total - 1).reshape(-1)
    halo_rows = REACH * block_size

    def extend(vectors):
        before, after = halo(vectors, "rows", halo_rows)
        outgoing = (
            vectors.reshape(block_rows, block_size, sub_width)[local_index]
            * valid_mask[:, None, None]
        )
        remote = partner(outgoing.reshape(slot_total * block_size, sub_width), "rows", swap_level)
        return jnp.concatenate([before, vectors, after, remote], axis=0)

    first_term = block_apply(0, entries, positions, hamiltonian, extend(subspace), subspace)
    return block_apply(1, entries, positions, hamiltonian, extend(first_term), first_term, subspace)


def solution(mesh):
    placed = (P("rows", None), P("rows", None), P("rows", None), P("rows", None))
    return jax.shard_map(
        per_device, mesh=mesh, in_specs=placed, out_specs=P("rows", None), check_vma=False
    )
```

time: 119 us -> 73.1 us (0.61)
  the two profiles are of different devices: /device:TPU:1 before, /device:TPU:0 now
where the time goes in v1:
time: 73.1 us; the launch traced here: 72.7 us
  Pallas kernels  30.5 us (42%)
  starting transfers between devices  16.9 us (23%)
  local copies, waits for them, and re-layouts  14.3 us (20%)
  waiting for transfers between devices  10.2 us (14%)
    pallas_call x2, Pallas kernels, block_apply(): pl.pallas_call(functools.partial(apply_kernel, mode, entries, block_size)...  30.5 us
    ppermute x2, starting transfers between devices, halo(): after = lax.ppermute(value[:width], axis, down)  14.9 us
    unnamed x5, local copies, waits for them, and re-layouts  11.7 us
    ppermute x3, waiting for transfers between devices, partner(): return lax.ppermute(value, axis, pairs)  10.1 us
    ppermute x3, starting transfers between devices, partner(): return lax.ppermute(value, axis, pairs)  1.82 us
  transfers between devices with their start and end apart: 7, of which 1 were waited for; matrix products, arithmetic and copies ran while one was open for 19% of the time, Pallas kernels for 0%

profile of v1, /device:TPU:0, one launch (start us, length us, event | category | flops | bytes accessed | tf_op | source)
XLA Modules:
  0.0 72.7 jit_solution(7741037914841936222)
XLA Ops:
  0.0 1.5 %collective-permute-start.2 = (s32[1,8]{1,0:T(1,128)}, s32[1,8]{1,0:T(1,128)S(1)}, u32[]{:S(2)}, u32[]{:S(2)}) collective-permute-start(s32[1,8]{1,0:T(1,128)} %param.7), channel_id=1, source_target_pairs={{0,32},{1,33},{2,34},{3,35},{4,36},{5,37},{6,38},{7,39},{8,40},{9,... | collective-permute-start | bytes 104 | tf_op jit(solution)/shard_map/ppermute | solution.py:19
  1.5 1.2 %fusion.8 = (f32[832,128]{1,0:T(8,128)S(1)}, f32[832,128]{1,0:T(8,128)S(1)}) fusion(f32[1536,128]{1,0:T(8,128)} %rest_0_.1), kind=kLoop, calls=%fused_computation.19 | loop fusion | bytes 1703936 | tf_op jit(solution)/shard_map/slice | solution.py:26
  2.7 0.1 collective-permute-start
  2.7 7.8 %collective-permute-start.1 = (f32[832,128]{1,0:T(8,128)S(1)}, f32[832,128]{1,0:T(8,128)S(1)}, u32[]{:S(2)}, u32[]{:S(2)}) collective-permute-start(f32[832,128]{1,0:T(8,128)S(1)} %get-tuple-element.8), channel_id=1, source_target_pairs={{1,0},{2,1},{3,2},{4,3},{5,4},{6,5},{7,6},{8,7},{9,8},{10,9},{11,1... | collective-permute-start | bytes 1277960 | tf_op jit(solution)/shard_map/ppermute | solution.py:27
  10.5 0.0 collective-permute-done.2
  10.6 0.1 mul.24
  10.6 0.1 mul.25
  10.7 0.6 gather_fusion
  11.3 0.1 bitcast_multiply_fusion.1
  11.4 0.1 collective-permute-start.3
  11.6 0.1 reshape.52.pos_ref
  11.7 11.7 %copy.6.ham_ref = f32[1536,1728]{1,0:T(8,128)} copy(f32[1536,1728]{0,1:T(8,128)} %param.4) | data formatting | bytes 21233664 | tf_op args[0]
  23.4 0.0 collective-permute-done.3
  23.4 0.1 pad_maximum_fusion.ext_ref
  23.5 14.9 %shard_map.46.own_ref = f32[1536,128]{1,0:T(8,128)S(1)} custom-call(s32[648]{0:T(1024)S(1)} %reshape.52.pos_ref, f32[1536,1728]{1,0:T(8,128)} %copy.6.ham_ref, f32[3712,128]{1,0:T(8,128)S(1)} %pad_maximum_fusion.ext_ref, f32[1536,128]{1,0:T(8,128)S(1)} %copy-done), custom_call_target="tpu_custom_call" | custom-call | flops 4076863488 | bytes 14876672 | tf_op jit(solution)/shard_map/pallas_call | solution.py:75
  38.4 0.1 fusion.7
  38.5 0.6 gather_fusion.1
  39.1 0.1 collective-permute-start.4
  39.2 7.2 %collective-permute-start.5 = (f32[832,128]{1,0:T(8,128)S(1)}, f32[832,128]{1,0:T(8,128)S(1)}, u32[]{:S(2)}, u32[]{:S(2)}) collective-permute-start(f32[832,128]{1,0:T(8,128)S(1)} %get-tuple-element.6), channel_id=1, source_target_pairs={{1,0},{2,1},{3,2},{4,3},{5,4},{6,5},{7,6},{8,7},{9,8},{10,9},{11,1... | collective-permute-start | bytes 1277960 | tf_op jit(solution)/shard_map/ppermute | solution.py:27
  46.3 0.1 bitcast_multiply_fusion
  46.5 0.3 collective-permute-start.6
  46.7 10.1 %collective-permute-done.6 = f32[512,128]{1,0:T(8,128)S(1)} collective-permute-done((f32[512,128]{1,0:T(8,128)S(1)}, f32[512,128]{1,0:T(8,128)S(1)}, u32[]{:S(2)}, u32[]{:S(2)}) %collective-permute-start.6) | collective-permute-done | bytes 262176 | tf_op jit(solution)/shard_map/ppermute | solution.py:19
  56.9 0.1 pad_maximum_fusion.1.ext_ref
  57.0 15.7 %shard_map.47 = f32[1536,128]{1,0:T(8,128)} custom-call(s32[648]{0:T(1024)S(1)} %reshape.52.pos_ref, f32[1536,1728]{1,0:T(8,128)} %copy.6.ham_ref, f32[3712,128]{1,0:T(8,128)S(1)} %pad_maximum_fusion.1.ext_ref, f32[1536,128]{1,0:T(8,128)S(1)} %shard_map.46.own_ref, f32[1536,128]{1,0:T(8,128)S(1)} %copy-done), custom_call_target="tpu_custom_call" | custom-call | flops 4076863488 | bytes 14876672 | tf_op jit(solution)/shard_map/pallas_call | solution.py:75
  (12 shorter events, 0.1 us)
Async XLA Ops:
  0.0 10.7 %copy-start = (f32[1536,128]{1,0:T(8,128)S(1)}, f32[1536,128]{1,0:T(8,128)}, u32[]{:S(2)}) copy-start(f32[1536,128]{1,0:T(8,128)} %rest_0_.1) | copy-start | bytes 2359300
  0.0 11.5 %copy-start.1 = (s32[24,27]{1,0:T(8,128)S(1)}, s32[24,27]{1,0:T(8,128)}, u32[]{:S(2)}) copy-start(s32[24,27]{1,0:T(8,128)} %param.6) | copy-start | bytes 7780
  0.0 10.5 %collective-permute-start.2 = (s32[1,8]{1,0:T(1,128)}, s32[1,8]{1,0:T(1,128)S(1)}, u32[]{:S(2)}, u32[]{:S(2)}) collective-permute-start(s32[1,8]{1,0:T(1,128)} %param.7), channel_id=1, source_target_pairs={{0,32},{1,33},{2,34},{3,35},{4,36},{5,37},{6,38},{7,39},{8,40},{9,... | collective-permute-start | bytes 104 | tf_op jit(solution)/shard_map/ppermute | solution.py:19
  2.7 20.7 %collective-permute-start = (f32[832,128]{1,0:T(8,128)S(1)}, f32[832,128]{1,0:T(8,128)S(1)}, u32[]{:S(2)}, u32[]{:S(2)}) collective-permute-start(f32[832,128]{1,0:T(8,128)S(1)} %get-tuple-element.7), channel_id=1, source_target_pairs={{0,1},{1,2},{2,3},{3,4},{4,5},{5,6},{6,7},{7,8},{8,9},{9,10},{10,1... | collective-permute-start | bytes 1277960 | tf_op jit(solution)/shard_map/ppermute | solution.py:26
  2.7 20.6 %collective-permute-start.1 = (f32[832,128]{1,0:T(8,128)S(1)}, f32[832,128]{1,0:T(8,128)S(1)}, u32[]{:S(2)}, u32[]{:S(2)}) collective-permute-start(f32[832,128]{1,0:T(8,128)S(1)} %get-tuple-element.8), channel_id=1, source_target_pairs={{1,0},{2,1},{3,2},{4,3},{5,4},{6,5},{7,6},{8,7},{9,8},{10,9},{11,1... | collective-permute-start | bytes 1277960 | tf_op jit(solution)/shard_map/ppermute | solution.py:27
  11.4 12.0 %collective-permute-start.3 = (f32[512,128]{1,0:T(8,128)S(1)}, f32[512,128]{1,0:T(8,128)S(1)}, u32[]{:S(2)}, u32[]{:S(2)}) collective-permute-start(f32[512,128]{1,0:T(8,128)S(1)} %bitcast_multiply_fusion.1), channel_id=1, source_target_pairs={{0,32},{1,33},{2,34},{3,35},{4,36},{5,37},{6,38},{7,39},{8,40},{9,... | collective-permute-start | bytes 786440 | tf_op jit(solution)/shard_map/ppermute | solution.py:19
  39.1 17.8 %collective-permute-start.4 = (f32[832,128]{1,0:T(8,128)S(1)}, f32[832,128]{1,0:T(8,128)S(1)}, u32[]{:S(2)}, u32[]{:S(2)}) collective-permute-start(f32[832,128]{1,0:T(8,128)S(1)} %get-tuple-element.5), channel_id=1, source_target_pairs={{0,1},{1,2},{2,3},{3,4},{4,5},{5,6},{6,7},{7,8},{8,9},{9,10},{10,1... | collective-permute-start | bytes 1277960 | tf_op jit(solution)/shard_map/ppermute | solution.py:26
  39.2 17.7 %collective-permute-start.5 = (f32[832,128]{1,0:T(8,128)S(1)}, f32[832,128]{1,0:T(8,128)S(1)}, u32[]{:S(2)}, u32[]{:S(2)}) collective-permute-start(f32[832,128]{1,0:T(8,128)S(1)} %get-tuple-element.6), channel_id=1, source_target_pairs={{1,0},{2,1},{3,2},{4,3},{5,4},{6,5},{7,6},{8,7},{9,8},{10,9},{11,1... | collective-permute-start | bytes 1277960 | tf_op jit(solution)/shard_map/ppermute | solution.py:27
  46.5 10.4 %collective-permute-start.6 = (f32[512,128]{1,0:T(8,128)S(1)}, f32[512,128]{1,0:T(8,128)S(1)}, u32[]{:S(2)}, u32[]{:S(2)}) collective-permute-start(f32[512,128]{1,0:T(8,128)S(1)} %bitcast_multiply_fusion), channel_id=1, source_target_pairs={{0,32},{1,33},{2,34},{3,35},{4,36},{5,37},{6,38},{7,39},{8,40},{9,... | collective-permute-start | bytes 786440 | tf_op jit(solution)/shard_map/ppermute | solution.py:19

commit v2 on v1

--- a/solution.py
+++ b/solution.py
@@ -28,13 +28,29 @@
     return before, after
 
 
+def split(x):
+    hi = x.astype(jnp.bfloat16)
+    return hi, (x - hi.astype(jnp.float32)).astype(jnp.bfloat16)
+
+
+def split_dot(transposed, panel):
+    numbers = (((0,), (0,)), ((), ()))
+    th, tl = split(transposed)
+    ph, pw = split(panel)
+
+    def dot(a, b):
+        return lax.dot_general(a, b, numbers, preferred_element_type=jnp.float32)
+
+    return dot(th, ph) + (dot(th, pw) + dot(tl, ph))
+
+
 def apply_kernel(mode, entries, block_size, pos_ref, ham_ref, ext_ref, own_ref, *rest):
     if mode == 0:
         (out_ref,) = rest
     else:
         base_ref, out_ref = rest
     step = pl.program_id(0)
-    rows = ham_ref.shape[0] // block_size
+    rows = ham_ref.shape[1] // block_size
     for r in range(rows):
         i = step * rows + r
         pieces = []
@@ -42,12 +58,7 @@
             start = pl.multiple_of(pos_ref[i * entries + j] * block_size, block_size)
             pieces.append(ext_ref[pl.ds(start, block_size), :])
         panel = jnp.concatenate(pieces, axis=0)
-        acc = jnp.dot(
-            ham_ref[r * block_size:(r + 1) * block_size, :],
-            panel,
-            precision=lax.Precision.HIGHEST,
-            preferred_element_type=jnp.float32,
-        )
+        acc = split_dot(ham_ref[:, r * block_size:(r + 1) * block_size], panel)
         rs = slice(r * block_size, (r + 1) * block_size)
         own = own_ref[rs, :]
         if mode == 0:
@@ -56,22 +67,22 @@
             out_ref[rs, :] = 2.0 / HALF_WIDTH * (acc - CENTER * own) - base_ref[rs, :]
 
 
-def block_apply(mode, entries, positions, hamiltonian, extended, own, base=None):
-    block_size = hamiltonian.shape[1] // entries
+def block_apply(mode, entries, positions, transposed, extended, own, base=None):
+    block_size = transposed.shape[0] // entries
     block_rows = own.shape[0] // block_size
     step_rows = ROWS_PER_STEP * block_size
     steps = block_rows // ROWS_PER_STEP
     width = own.shape[1]
     in_specs = [
-        pl.BlockSpec((step_rows, hamiltonian.shape[1]), lambda s, pos: (s, 0)),
+        pl.BlockSpec((transposed.shape[0], step_rows), lambda s, pos: (0, s)),
         pl.BlockSpec(extended.shape, lambda s, pos: (0, 0)),
         pl.BlockSpec((step_rows, width), lambda s, pos: (s, 0)),
     ]
-    args = [hamiltonian, extended, own]
+    args = [transposed, extended, own]
     if mode == 1:
         in_specs.append(pl.BlockSpec((step_rows, width), lambda s, pos: (s, 0)))
         args.append(base)
-    flops = 2 * hamiltonian.shape[0] * hamiltonian.shape[1] * width
+    flops = 2 * transposed.shape[0] * transposed.shape[1] * width
     return pl.pallas_call(
         functools.partial(apply_kernel, mode, entries, block_size),
         out_shape=jax.ShapeDtypeStruct(own.shape, jnp.float32),
@@ -83,9 +94,9 @@
         ),
         compiler_params=pltpu.CompilerParams(vmem_limit_bytes=48 * 1024 * 1024),
         cost_estimate=pl.CostEstimate(
-            flops=6 * flops,
+            flops=3 * flops,
             transcendentals=0,
-            bytes_accessed=4 * (hamiltonian.size + extended.size + 3 * own.size),
+            bytes_accessed=4 * (transposed.size + extended.size + 3 * own.size),
         ),
     )(positions, *args)
 
@@ -121,8 +132,9 @@
         remote = partner(outgoing.reshape(slot_total * block_size, sub_width), "rows", swap_level)
         return jnp.concatenate([before, vectors, after, remote], axis=0)
 
-    first_term = block_apply(0, entries, positions, hamiltonian, extend(subspace), subspace)
-    return block_apply(1, entries, positions, hamiltonian, extend(first_term), first_term, subspace)
+    transposed = hamiltonian.T
+    first_term = block_apply(0, entries, positions, transposed, extend(subspace), subspace)
+    return block_apply(1, entries, positions, transposed, extend(first_term), first_term, subspace)
 
 
 def solution(mesh):

time: 73.1 us -> 68 us (0.930)
  local copies, waits for them, and re-layouts: 14.3 us -> 2.62 us
  waiting for transfers between devices: 10.2 us -> 18.4 us
  Pallas kernels: 30.5 us -> 28.5 us
    unnamed x5 -> x4, local copies, waits for them, and re-layouts: 11.7 us -> 0.01 us
    ppermute x3, waiting for transfers between devices: 10.1 us -> 18.4 us  [partner(): return lax.ppermute(value, axis, pairs)]
    pallas_call x2, Pallas kernels: 30.5 us -> 28.5 us  [block_apply(): pl.pallas_call(functools.partial(apply_kernel, mode, entries, block_size)...]
  transfers between devices with their start and end apart: 7 -> 7, of which waited for: 1 -> 2; matrix products, arithmetic and copies ran while one was open for 19% -> 3% of each run, Pallas kernels for 0% -> 0%
where the time goes in v2:
time: 68 us; the launch traced here: 67.1 us
  Pallas kernels  28.5 us (42%)
  waiting for transfers between devices  18.4 us (27%)
  starting transfers between devices  16.8 us (25%)
  local copies, waits for them, and re-layouts  2.62 us (4%)
    pallas_call x2, Pallas kernels, block_apply(): pl.pallas_call(functools.partial(apply_kernel, mode, entries, block_size)...  28.5 us
    ppermute x3, waiting for transfers between devices, partner(): return lax.ppermute(value, axis, pairs)  18.4 us
    ppermute x2, starting transfers between devices, halo(): after = lax.ppermute(value[:width], axis, down)  15 us
    ppermute x3, starting transfers between devices, partner(): return lax.ppermute(value, axis, pairs)  1.64 us
  transfers between devices with their start and end apart: 7, of which 2 were waited for; matrix products, arithmetic and copies ran while one was open for 3% of the time, Pallas kernels for 0%

profile of v2, /device:TPU:0, one launch (start us, length us, event | category | flops | bytes accessed | tf_op | source)
XLA Modules:
  0.0 67.1 jit_solution(14127121359601710022)
XLA Ops:
  0.0 1.5 %collective-permute-start.2 = (s32[1,8]{1,0:T(1,128)}, s32[1,8]{1,0:T(1,128)S(1)}, u32[]{:S(2)}, u32[]{:S(2)}) collective-permute-start(s32[1,8]{1,0:T(1,128)} %param.7), channel_id=1, source_target_pairs={{0,32},{1,33},{2,34},{3,35},{4,36},{5,37},{6,38},{7,39},{8,40},{9,... | collective-permute-start | bytes 104 | tf_op jit(solution)/shard_map/ppermute | solution.py:19
  1.5 1.2 %fusion.8 = (f32[832,128]{1,0:T(8,128)S(1)}, f32[832,128]{1,0:T(8,128)S(1)}) fusion(f32[1536,128]{1,0:T(8,128)} %rest_0_.1), kind=kLoop, calls=%fused_computation.19 | loop fusion | bytes 1703936 | tf_op jit(solution)/shard_map/slice | solution.py:26
  2.7 0.1 collective-permute-start
  2.7 7.8 %collective-permute-start.1 = (f32[832,128]{1,0:T(8,128)S(1)}, f32[832,128]{1,0:T(8,128)S(1)}, u32[]{:S(2)}, u32[]{:S(2)}) collective-permute-start(f32[832,128]{1,0:T(8,128)S(1)} %get-tuple-element.8), channel_id=1, source_target_pairs={{1,0},{2,1},{3,2},{4,3},{5,4},{6,5},{7,6},{8,7},{9,8},{10,9},{11,1... | collective-permute-start | bytes 1277960 | tf_op jit(solution)/shard_map/ppermute | solution.py:27
  10.5 0.0 collective-permute-done.2
  10.6 0.1 mul.24
  10.6 0.1 mul.25
  10.7 0.6 gather_fusion
  11.3 0.1 bitcast_multiply_fusion.1
  11.4 0.1 collective-permute-start.3
  11.6 0.1 reshape.52.pos_ref
  11.7 10.1 %collective-permute-done.3 = f32[512,128]{1,0:T(8,128)S(1)} collective-permute-done((f32[512,128]{1,0:T(8,128)S(1)}, f32[512,128]{1,0:T(8,128)S(1)}, u32[]{:S(2)}, u32[]{:S(2)}) %collective-permute-start.3) | collective-permute-done | bytes 262176 | tf_op jit(solution)/shard_map/ppermute | solution.py:19
  21.8 0.0 collective-permute-done
  21.8 0.1 pad_maximum_fusion.ext_ref
  21.9 13.9 %shard_map.46.own_ref = f32[1536,128]{1,0:T(8,128)S(1)} custom-call(s32[648]{0:T(1024)S(1)} %reshape.52.pos_ref, f32[1728,1536]{1,0:T(8,128)} %bitcast.15, f32[3712,128]{1,0:T(8,128)S(1)} %pad_maximum_fusion.ext_ref, f32[1536,128]{1,0:T(8,128)S(1)} %copy-done), custom_call_target="tpu_custom_call" | custom-call | flops 2038431744 | bytes 14876672 | tf_op jit(solution)/shard_map/pallas_call | solution.py:86
  35.9 0.1 fusion.7
  35.9 0.6 gather_fusion.1
  36.5 0.1 collective-permute-start.4
  36.6 7.2 %collective-permute-start.5 = (f32[832,128]{1,0:T(8,128)S(1)}, f32[832,128]{1,0:T(8,128)S(1)}, u32[]{:S(2)}, u32[]{:S(2)}) collective-permute-start(f32[832,128]{1,0:T(8,128)S(1)} %get-tuple-element.6), channel_id=1, source_target_pairs={{1,0},{2,1},{3,2},{4,3},{5,4},{6,5},{7,6},{8,7},{9,8},{10,9},{11,1... | collective-permute-start | bytes 1277960 | tf_op jit(solution)/shard_map/ppermute | solution.py:27
  43.8 0.1 bitcast_multiply_fusion
  44.0 0.1 collective-permute-start.6
  44.1 8.3 %collective-permute-done.6 = f32[512,128]{1,0:T(8,128)S(1)} collective-permute-done((f32[512,128]{1,0:T(8,128)S(1)}, f32[512,128]{1,0:T(8,128)S(1)}, u32[]{:S(2)}, u32[]{:S(2)}) %collective-permute-start.6) | collective-permute-done | bytes 262176 | tf_op jit(solution)/shard_map/ppermute | solution.py:19
  52.4 0.1 pad_maximum_fusion.1.ext_ref
  52.5 14.6 %shard_map.47 = f32[1536,128]{1,0:T(8,128)} custom-call(s32[648]{0:T(1024)S(1)} %reshape.52.pos_ref, f32[1728,1536]{1,0:T(8,128)} %bitcast.16, f32[3712,128]{1,0:T(8,128)S(1)} %pad_maximum_fusion.1.ext_ref, f32[1536,128]{1,0:T(8,128)S(1)} %shard_map.46.own_ref, f32[1536,128]{1,0:T(8,128)S(1)} %copy-done), custom_call_target="tpu_custom_call" | custom-call | flops 2038431744 | bytes 14876672 | tf_op jit(solution)/shard_map/pallas_call | solution.py:86
  (11 shorter events, 0.1 us)
Async XLA Ops:
  0.0 10.7 %copy-start = (f32[1536,128]{1,0:T(8,128)S(1)}, f32[1536,128]{1,0:T(8,128)}, u32[]{:S(2)}) copy-start(f32[1536,128]{1,0:T(8,128)} %rest_0_.1) | copy-start | bytes 2359300
  0.0 11.5 %copy-start.1 = (s32[24,27]{1,0:T(8,128)S(1)}, s32[24,27]{1,0:T(8,128)}, u32[]{:S(2)}) copy-start(s32[24,27]{1,0:T(8,128)} %param.6) | copy-start | bytes 7780
  0.0 10.5 %collective-permute-start.2 = (s32[1,8]{1,0:T(1,128)}, s32[1,8]{1,0:T(1,128)S(1)}, u32[]{:S(2)}, u32[]{:S(2)}) collective-permute-start(s32[1,8]{1,0:T(1,128)} %param.7), channel_id=1, source_target_pairs={{0,32},{1,33},{2,34},{3,35},{4,36},{5,37},{6,38},{7,39},{8,40},{9,... | collective-permute-start | bytes 104 | tf_op jit(solution)/shard_map/ppermute | solution.py:19
  2.7 19.1 %collective-permute-start = (f32[832,128]{1,0:T(8,128)S(1)}, f32[832,128]{1,0:T(8,128)S(1)}, u32[]{:S(2)}, u32[]{:S(2)}) collective-permute-start(f32[832,128]{1,0:T(8,128)S(1)} %get-tuple-element.7), channel_id=1, source_target_pairs={{0,1},{1,2},{2,3},{3,4},{4,5},{5,6},{6,7},{7,8},{8,9},{9,10},{10,1... | collective-permute-start | bytes 1277960 | tf_op jit(solution)/shard_map/ppermute | solution.py:26
  2.7 19.0 %collective-permute-start.1 = (f32[832,128]{1,0:T(8,128)S(1)}, f32[832,128]{1,0:T(8,128)S(1)}, u32[]{:S(2)}, u32[]{:S(2)}) collective-permute-start(f32[832,128]{1,0:T(8,128)S(1)} %get-tuple-element.8), channel_id=1, source_target_pairs={{1,0},{2,1},{3,2},{4,3},{5,4},{6,5},{7,6},{8,7},{9,8},{10,9},{11,1... | collective-permute-start | bytes 1277960 | tf_op jit(solution)/shard_map/ppermute | solution.py:27
  11.4 10.3 %collective-permute-start.3 = (f32[512,128]{1,0:T(8,128)S(1)}, f32[512,128]{1,0:T(8,128)S(1)}, u32[]{:S(2)}, u32[]{:S(2)}) collective-permute-start(f32[512,128]{1,0:T(8,128)S(1)} %bitcast_multiply_fusion.1), channel_id=1, source_target_pairs={{0,32},{1,33},{2,34},{3,35},{4,36},{5,37},{6,38},{7,39},{8,40},{9,... | collective-permute-start | bytes 786440 | tf_op jit(solution)/shard_map/ppermute | solution.py:19
  36.5 15.9 %collective-permute-start.4 = (f32[832,128]{1,0:T(8,128)S(1)}, f32[832,128]{1,0:T(8,128)S(1)}, u32[]{:S(2)}, u32[]{:S(2)}) collective-permute-start(f32[832,128]{1,0:T(8,128)S(1)} %get-tuple-element.5), channel_id=1, source_target_pairs={{0,1},{1,2},{2,3},{3,4},{4,5},{5,6},{6,7},{7,8},{8,9},{9,10},{10,1... | collective-permute-start | bytes 1277960 | tf_op jit(solution)/shard_map/ppermute | solution.py:26
  36.6 15.8 %collective-permute-start.5 = (f32[832,128]{1,0:T(8,128)S(1)}, f32[832,128]{1,0:T(8,128)S(1)}, u32[]{:S(2)}, u32[]{:S(2)}) collective-permute-start(f32[832,128]{1,0:T(8,128)S(1)} %get-tuple-element.6), channel_id=1, source_target_pairs={{1,0},{2,1},{3,2},{4,3},{5,4},{6,5},{7,6},{8,7},{9,8},{10,9},{11,1... | collective-permute-start | bytes 1277960 | tf_op jit(solution)/shard_map/ppermute | solution.py:27
  44.0 8.4 %collective-permute-start.6 = (f32[512,128]{1,0:T(8,128)S(1)}, f32[512,128]{1,0:T(8,128)S(1)}, u32[]{:S(2)}, u32[]{:S(2)}) collective-permute-start(f32[512,128]{1,0:T(8,128)S(1)} %bitcast_multiply_fusion), channel_id=1, source_target_pairs={{0,32},{1,33},{2,34},{3,35},{4,36},{5,37},{6,38},{7,39},{8,40},{9,... | collective-permute-start | bytes 786440 | tf_op jit(solution)/shard_map/ppermute | solution.py:19
